TPU v7x, 32 devices: a whole 2x2x4 slice. The times are simulated.
32 devices in a mesh: cols: 16 (over z, y, x), params: 2 (over core).
Axes of the slice: x: 2, y: 2, z: 4, core: 2. Of those that a mesh axis runs over, the one named last changes fastest.
Arguments:
- concentration: float32 [128, 16384], P(None, ('cols', 'params')), may hold values from 0.2 to 5
- emissions: float32 [128, 16384], P(None, ('cols', 'params')), may hold values from 0 to 1
- rate_table: float32 [8, 16, 16], replicated, may hold values from 0.01 to 0.3
- species_order: int32 [128], replicated, may hold values from 0 to 127, each once
- sensitivity: float32 [4, 128, 32, 4, 128], P('params', None, 'cols'), may hold values from -6 to 6
- source_terms: bfloat16 [4, 128, 32, 4, 128], P('params', None, 'cols'), may hold values from 0 to 2
- courant_x: float32 [32, 4, 128], P('cols'), may hold values from 0.05 to 0.24
- upwind_x: int32 [32, 4, 128], P('cols'), may hold values from 0 to 1
- courant_y: float32 [32, 4, 128], P('cols'), may hold values from 0.05 to 0.24
- upwind_y: int32 [32, 4, 128], P('cols'), may hold values from 0 to 1
Outputs:
- new_concentration: float32 [128, 16384], P(None, ('cols', 'params'))
- new_sensitivity: float32 [4, 128, 32, 4, 128], P('params', None, 'cols')
- sensitivity_burden: float32 [4, 128], P('params')
- species_burden: float32 [128], replicated
Inputs may be any that keep to these rules, and one draw needn't show every extreme that they name: `species_order`: each species appears exactly once. `upwind_x`: 1 means the wind blows toward higher indices through the face. `upwind_y`: 1 means the wind blows toward higher indices through the face.
All inputs are finite; a program needn't handle non-finite values.
Results may differ from a plain program's by a relative error of at most 0.0016.
Values may be sent and summed in bfloat16 or wider, within the bound.
A program may use at most 128 MiB of HBM per device.

v0:
```python
import jax
import jax.numpy as jnp
from jax import lax
from jax.sharding import PartitionSpec as P

SUBSTEPS = 2


def for_sending(value):

    def short(part):
        return part.astype(jnp.bfloat16) if part.dtype == jnp.float32 else part

    return jax.tree.map(short, value)


def passed_along(value, axis, by):
    devices = lax.axis_size(axis)
    pairs = [(i, i + by) for i in range(devices) if 0 <= i + by < devices]
    return lax.ppermute(value, axis, pairs)


def invert_blocks(matrix):
    size = matrix.shape[1]
    positions = jnp.arange(size)

    def eliminate(pivot_index, current):
        pivot = 1.0 / current[:, pivot_index, pivot_index, :]
        pivot_row = current[:, pivot_index, :, :] * pivot[:, None, :]
        pivot_row = jnp.where(
            (positions == pivot_index)[None, :, None], pivot[:, None, :], pivot_row
        )
        column = current[:, :, pivot_index, :]
        updated = current - column[:, :, None, :] * pivot_row[:, None, :, :]
        updated = jnp.where(
            (positions == pivot_index)[None, None, :, None],
            -column[:, :, None, :] * pivot[:, None, None, :],
            updated,
        )
        updated = jnp.where(
            (positions == pivot_index)[None, :, None, None], pivot_row[:, None, :, :], updated
        )
        return updated

    return lax.fori_loop(0, size, eliminate, matrix)


def build_factors(conc_cells, species_order, rate_table):
    block_count, block_width = (rate_table.shape[0], rate_table.shape[1])
    ordered = jnp.take(conc_cells, species_order, axis=0).reshape(block_count, block_width, -1)
    coupling = rate_table[:, :, :, None] * ordered[:, None, :, :]
    row_total = jnp.sum(coupling, axis=2)
    positions = jnp.arange(block_width)
    identity = (positions[:, None] == positions[None, :]).astype(jnp.float32)
    system = identity[None, :, :, None] * (1.0 + row_total)[:, :, None, :] - coupling
    return invert_blocks(system).astype(jnp.bfloat16)


def apply_blocks(factors, values):
    result = jnp.zeros(values.shape, jnp.float32)
    for column_index in range(factors.shape[2]):
        result = (
            result
            + factors[:, :, column_index, :].astype(jnp.float32)[None]
            * values[:, :, column_index, :][:, :, None, :]
        )
    return result


def across_flux(tracer, courant_y, upwind_y):
    before_y = jnp.concatenate([jnp.zeros_like(tracer[..., :1]), tracer[..., :-1]], axis=4)
    lower_y = courant_y * jnp.where(upwind_y == 1, before_y, -tracer)
    upper_y = jnp.concatenate([lower_y[..., 1:], jnp.zeros_like(lower_y[..., :1])], axis=4)
    return lower_y - upper_y


def advect(tracer, courant_x, upwind_x, courant_y, upwind_y):
    left_plane = passed_along(for_sending(tracer[:, :, -1:]), "cols", 1)
    before_x = jnp.concatenate([left_plane, tracer[:, :, :-1]], axis=2)
    lower_x = courant_x * jnp.where(upwind_x == 1, before_x, -tracer)
    right_plane = passed_along(for_sending(lower_x[:, :, :1]), "cols", -1)
    upper_x = jnp.concatenate([lower_x[:, :, 1:], right_plane], axis=2)
    return tracer + lower_x - upper_x + across_flux(tracer, courant_y, upwind_y)


def shards(
    concentration,
    emissions,
    rate_table,
    species_order,
    sensitivity,
    source_terms,
    courant_x,
    upwind_x,
    courant_y,
    upwind_y,
):
    block_count, block_width = (rate_table.shape[0], rate_table.shape[1])
    groups, species = (sensitivity.shape[0], sensitivity.shape[1])
    planes, layers, across = (sensitivity.shape[2], sensitivity.shape[3], sensitivity.shape[4])
    cell_count = planes * layers * across
    inverse = jnp.argsort(species_order)
    own_factors = build_factors(concentration, species_order, rate_table)
    base_side = jnp.take(concentration + emissions, species_order, axis=0).reshape(
        block_count, block_width, -1
    )
    new_base = apply_blocks(own_factors, base_side[None])[0].reshape(species, -1)
    new_concentration = jnp.take(new_base, inverse, axis=0)
    tracer = sensitivity
    for substep in range(SUBSTEPS):
        tracer = advect(tracer, courant_x, upwind_x, courant_y, upwind_y)
    right_side = jnp.take(tracer + source_terms.astype(jnp.float32), species_order, axis=1)
    right_side = right_side.reshape(groups, block_count, block_width, cell_count)
    result = apply_blocks(lax.all_gather(own_factors, "params", axis=3, tiled=True), right_side)
    new_sensitivity = jnp.take(
        result.reshape(groups, species, planes, layers, across), inverse, axis=1
    )
    partial_sens = jnp.sum(new_sensitivity, axis=(2, 3, 4))
    partial_conc = jnp.sum(new_concentration, axis=1)
    total_cells = cell_count * lax.axis_size("cols")
    group_index = lax.axis_index("params")
    row_table = jnp.zeros((groups * lax.axis_size("params"), species), jnp.float32)
    row_table = lax.dynamic_update_slice(row_table, partial_sens, (group_index * groups, 0))
    table_total, conc_total = lax.psum((row_table, partial_conc), ("cols", "params"))
    sens_total = lax.dynamic_slice(table_total, (group_index * groups, 0), (groups, species))
    return (new_concentration, new_sensitivity, sens_total / total_cells, conc_total / total_cells)


def solution(mesh):
    in_specs = (
        P(None, ("cols", "params")),
        P(None, ("cols", "params")),
        P(),
        P(),
        P("params", None, "cols", None, None),
        P("params", None, "cols", None, None),
        P("cols", None, None),
        P("cols", None, None),
        P("cols", None, None),
        P("cols", None, None),
    )
    out_specs = (
        P(None, ("cols", "params")),
        P("params", None, "cols", None, None),
        P("params", None),
        P(),
    )
    return jax.shard_map(shards, mesh=mesh, in_specs=in_specs, out_specs=out_specs, check_vma=False)
```

profile of v0, /device:TPU:0, one launch (start us, length us, event | category | flops | bytes accessed | tf_op | source)
XLA Modules:
  0.0 349.7 jit_solution(16836673207462641334)
XLA Ops:
  11.6 2.5 sort.17
  15.8 2.5 multiply_subtract_fusion
  18.4 151.3 %while.14 = (s32[]{:T(128)}, f32[8,16,16,512]{3,2,1,0:T(8,128)}, s32[]{:T(128)}) while((s32[]{:T(128)}, f32[8,16,16,512]{3,2,1,0:T(8,128)}, s32[]{:T(128)}) %tuple.112), condition=%wide.region_2.4_spmd.clone, body=%wide.region_1.3_spmd.clone.sunk | while | flops 4460562 | bytes 11632757 | solution.py:45
  19.3 2.0 negate_multiply_fusion.2
  22.5 5.3 %select_select_fusion.2 = f32[8,16,16,512]{3,2,1,0:T(8,128)} fusion(f32[8,16,16,512]{3,2,1,0:T(8,128)} %get-tuple-element.200, f32[8,16,512]{2,1,0:T(8,128)S(1)} %get-tuple-element.194, f32[8,16,512]{2,1,0:T(8,128)S(1)} %get-tuple-element.195, f32[8,16,512]{2,1,0:T(8,128)S(1)} %select_bitcast_fusion.5, pred[16]{0:T(512)(128)(4,1)S(1)} %iota_compare_fusion.3), kind=kLoop, calls=%fused_computation.6.clone.1 | loop fusion | flops 4194304 | bytes 9175056 | tf_op jit(solution)/shard_map/while/body/eval_jaxpr/jit(_where)/select_n | solution.py:40
  31.9 5.3 %select_select_fusion.2 = f32[8,16,16,512]{3,2,1,0:T(8,128)} fusion(f32[8,16,16,512]{3,2,1,0:T(8,128)} %get-tuple-element.200, f32[8,16,512]{2,1,0:T(8,128)S(1)} %get-tuple-element.194, f32[8,16,512]{2,1,0:T(8,128)S(1)} %get-tuple-element.195, f32[8,16,512]{2,1,0:T(8,128)S(1)} %select_bitcast_fusion.5, pred[16]{0:T(512)(128)(4,1)S(1)} %iota_compare_fusion.3), kind=kLoop, calls=%fused_computation.6.clone.1 | loop fusion | flops 4194304 | bytes 9175056 | tf_op jit(solution)/shard_map/while/body/eval_jaxpr/jit(_where)/select_n | solution.py:40
  41.4 5.3 %select_select_fusion.2 = f32[8,16,16,512]{3,2,1,0:T(8,128)} fusion(f32[8,16,16,512]{3,2,1,0:T(8,128)} %get-tuple-element.200, f32[8,16,512]{2,1,0:T(8,128)S(1)} %get-tuple-element.194, f32[8,16,512]{2,1,0:T(8,128)S(1)} %get-tuple-element.195, f32[8,16,512]{2,1,0:T(8,128)S(1)} %select_bitcast_fusion.5, pred[16]{0:T(512)(128)(4,1)S(1)} %iota_compare_fusion.3), kind=kLoop, calls=%fused_computation.6.clone.1 | loop fusion | flops 4194304 | bytes 9175056 | tf_op jit(solution)/shard_map/while/body/eval_jaxpr/jit(_where)/select_n | solution.py:40
  50.8 5.3 %select_select_fusion.2 = f32[8,16,16,512]{3,2,1,0:T(8,128)} fusion(f32[8,16,16,512]{3,2,1,0:T(8,128)} %get-tuple-element.200, f32[8,16,512]{2,1,0:T(8,128)S(1)} %get-tuple-element.194, f32[8,16,512]{2,1,0:T(8,128)S(1)} %get-tuple-element.195, f32[8,16,512]{2,1,0:T(8,128)S(1)} %select_bitcast_fusion.5, pred[16]{0:T(512)(128)(4,1)S(1)} %iota_compare_fusion.3), kind=kLoop, calls=%fused_computation.6.clone.1 | loop fusion | flops 4194304 | bytes 9175056 | tf_op jit(solution)/shard_map/while/body/eval_jaxpr/jit(_where)/select_n | solution.py:40
  60.3 5.3 %select_select_fusion.2 = f32[8,16,16,512]{3,2,1,0:T(8,128)} fusion(f32[8,16,16,512]{3,2,1,0:T(8,128)} %get-tuple-element.200, f32[8,16,512]{2,1,0:T(8,128)S(1)} %get-tuple-element.194, f32[8,16,512]{2,1,0:T(8,128)S(1)} %get-tuple-element.195, f32[8,16,512]{2,1,0:T(8,128)S(1)} %select_bitcast_fusion.5, pred[16]{0:T(512)(128)(4,1)S(1)} %iota_compare_fusion.3), kind=kLoop, calls=%fused_computation.6.clone.1 | loop fusion | flops 4194304 | bytes 9175056 | tf_op jit(solution)/shard_map/while/body/eval_jaxpr/jit(_where)/select_n | solution.py:40
  69.8 5.3 %select_select_fusion.2 = f32[8,16,16,512]{3,2,1,0:T(8,128)} fusion(f32[8,16,16,512]{3,2,1,0:T(8,128)} %get-tuple-element.200, f32[8,16,512]{2,1,0:T(8,128)S(1)} %get-tuple-element.194, f32[8,16,512]{2,1,0:T(8,128)S(1)} %get-tuple-element.195, f32[8,16,512]{2,1,0:T(8,128)S(1)} %select_bitcast_fusion.5, pred[16]{0:T(512)(128)(4,1)S(1)} %iota_compare_fusion.3), kind=kLoop, calls=%fused_computation.6.clone.1 | loop fusion | flops 4194304 | bytes 9175056 | tf_op jit(solution)/shard_map/while/body/eval_jaxpr/jit(_where)/select_n | solution.py:40
  79.2 5.3 %select_select_fusion.2 = f32[8,16,16,512]{3,2,1,0:T(8,128)} fusion(f32[8,16,16,512]{3,2,1,0:T(8,128)} %get-tuple-element.200, f32[8,16,512]{2,1,0:T(8,128)S(1)} %get-tuple-element.194, f32[8,16,512]{2,1,0:T(8,128)S(1)} %get-tuple-element.195, f32[8,16,512]{2,1,0:T(8,128)S(1)} %select_bitcast_fusion.5, pred[16]{0:T(512)(128)(4,1)S(1)} %iota_compare_fusion.3), kind=kLoop, calls=%fused_computation.6.clone.1 | loop fusion | flops 4194304 | bytes 9175056 | tf_op jit(solution)/shard_map/while/body/eval_jaxpr/jit(_where)/select_n | solution.py:40
  88.7 5.3 %select_select_fusion.2 = f32[8,16,16,512]{3,2,1,0:T(8,128)} fusion(f32[8,16,16,512]{3,2,1,0:T(8,128)} %get-tuple-element.200, f32[8,16,512]{2,1,0:T(8,128)S(1)} %get-tuple-element.194, f32[8,16,512]{2,1,0:T(8,128)S(1)} %get-tuple-element.195, f32[8,16,512]{2,1,0:T(8,128)S(1)} %select_bitcast_fusion.5, pred[16]{0:T(512)(128)(4,1)S(1)} %iota_compare_fusion.3), kind=kLoop, calls=%fused_computation.6.clone.1 | loop fusion | flops 4194304 | bytes 9175056 | tf_op jit(solution)/shard_map/while/body/eval_jaxpr/jit(_where)/select_n | solution.py:40
  98.1 5.3 %select_select_fusion.2 = f32[8,16,16,512]{3,2,1,0:T(8,128)} fusion(f32[8,16,16,512]{3,2,1,0:T(8,128)} %get-tuple-element.200, f32[8,16,512]{2,1,0:T(8,128)S(1)} %get-tuple-element.194, f32[8,16,512]{2,1,0:T(8,128)S(1)} %get-tuple-element.195, f32[8,16,512]{2,1,0:T(8,128)S(1)} %select_bitcast_fusion.5, pred[16]{0:T(512)(128)(4,1)S(1)} %iota_compare_fusion.3), kind=kLoop, calls=%fused_computation.6.clone.1 | loop fusion | flops 4194304 | bytes 9175056 | tf_op jit(solution)/shard_map/while/body/eval_jaxpr/jit(_where)/select_n | solution.py:40
  107.6 5.3 %select_select_fusion.2 = f32[8,16,16,512]{3,2,1,0:T(8,128)} fusion(f32[8,16,16,512]{3,2,1,0:T(8,128)} %get-tuple-element.200, f32[8,16,512]{2,1,0:T(8,128)S(1)} %get-tuple-element.194, f32[8,16,512]{2,1,0:T(8,128)S(1)} %get-tuple-element.195, f32[8,16,512]{2,1,0:T(8,128)S(1)} %select_bitcast_fusion.5, pred[16]{0:T(512)(128)(4,1)S(1)} %iota_compare_fusion.3), kind=kLoop, calls=%fused_computation.6.clone.1 | loop fusion | flops 4194304 | bytes 9175056 | tf_op jit(solution)/shard_map/while/body/eval_jaxpr/jit(_where)/select_n | solution.py:40
  117.0 5.3 %select_select_fusion.2 = f32[8,16,16,512]{3,2,1,0:T(8,128)} fusion(f32[8,16,16,512]{3,2,1,0:T(8,128)} %get-tuple-element.200, f32[8,16,512]{2,1,0:T(8,128)S(1)} %get-tuple-element.194, f32[8,16,512]{2,1,0:T(8,128)S(1)} %get-tuple-element.195, f32[8,16,512]{2,1,0:T(8,128)S(1)} %select_bitcast_fusion.5, pred[16]{0:T(512)(128)(4,1)S(1)} %iota_compare_fusion.3), kind=kLoop, calls=%fused_computation.6.clone.1 | loop fusion | flops 4194304 | bytes 9175056 | tf_op jit(solution)/shard_map/while/body/eval_jaxpr/jit(_where)/select_n | solution.py:40
  126.5 5.3 %select_select_fusion.2 = f32[8,16,16,512]{3,2,1,0:T(8,128)} fusion(f32[8,16,16,512]{3,2,1,0:T(8,128)} %get-tuple-element.200, f32[8,16,512]{2,1,0:T(8,128)S(1)} %get-tuple-element.194, f32[8,16,512]{2,1,0:T(8,128)S(1)} %get-tuple-element.195, f32[8,16,512]{2,1,0:T(8,128)S(1)} %select_bitcast_fusion.5, pred[16]{0:T(512)(128)(4,1)S(1)} %iota_compare_fusion.3), kind=kLoop, calls=%fused_computation.6.clone.1 | loop fusion | flops 4194304 | bytes 9175056 | tf_op jit(solution)/shard_map/while/body/eval_jaxpr/jit(_where)/select_n | solution.py:40
  135.9 5.3 %select_select_fusion.2 = f32[8,16,16,512]{3,2,1,0:T(8,128)} fusion(f32[8,16,16,512]{3,2,1,0:T(8,128)} %get-tuple-element.200, f32[8,16,512]{2,1,0:T(8,128)S(1)} %get-tuple-element.194, f32[8,16,512]{2,1,0:T(8,128)S(1)} %get-tuple-element.195, f32[8,16,512]{2,1,0:T(8,128)S(1)} %select_bitcast_fusion.5, pred[16]{0:T(512)(128)(4,1)S(1)} %iota_compare_fusion.3), kind=kLoop, calls=%fused_computation.6.clone.1 | loop fusion | flops 4194304 | bytes 9175056 | tf_op jit(solution)/shard_map/while/body/eval_jaxpr/jit(_where)/select_n | solution.py:40
  145.4 5.3 %select_select_fusion.2 = f32[8,16,16,512]{3,2,1,0:T(8,128)} fusion(f32[8,16,16,512]{3,2,1,0:T(8,128)} %get-tuple-element.200, f32[8,16,512]{2,1,0:T(8,128)S(1)} %get-tuple-element.194, f32[8,16,512]{2,1,0:T(8,128)S(1)} %get-tuple-element.195, f32[8,16,512]{2,1,0:T(8,128)S(1)} %select_bitcast_fusion.5, pred[16]{0:T(512)(128)(4,1)S(1)} %iota_compare_fusion.3), kind=kLoop, calls=%fused_computation.6.clone.1 | loop fusion | flops 4194304 | bytes 9175056 | tf_op jit(solution)/shard_map/while/body/eval_jaxpr/jit(_where)/select_n | solution.py:40
  154.8 5.3 %select_select_fusion.2 = f32[8,16,16,512]{3,2,1,0:T(8,128)} fusion(f32[8,16,16,512]{3,2,1,0:T(8,128)} %get-tuple-element.200, f32[8,16,512]{2,1,0:T(8,128)S(1)} %get-tuple-element.194, f32[8,16,512]{2,1,0:T(8,128)S(1)} %get-tuple-element.195, f32[8,16,512]{2,1,0:T(8,128)S(1)} %select_bitcast_fusion.5, pred[16]{0:T(512)(128)(4,1)S(1)} %iota_compare_fusion.3), kind=kLoop, calls=%fused_computation.6.clone.1 | loop fusion | flops 4194304 | bytes 9175056 | tf_op jit(solution)/shard_map/while/body/eval_jaxpr/jit(_where)/select_n | solution.py:40
  164.3 5.3 %select_select_fusion.2 = f32[8,16,16,512]{3,2,1,0:T(8,128)} fusion(f32[8,16,16,512]{3,2,1,0:T(8,128)} %get-tuple-element.200, f32[8,16,512]{2,1,0:T(8,128)S(1)} %get-tuple-element.194, f32[8,16,512]{2,1,0:T(8,128)S(1)} %get-tuple-element.195, f32[8,16,512]{2,1,0:T(8,128)S(1)} %select_bitcast_fusion.5, pred[16]{0:T(512)(128)(4,1)S(1)} %iota_compare_fusion.3), kind=kLoop, calls=%fused_computation.6.clone.1 | loop fusion | flops 4194304 | bytes 9175056 | tf_op jit(solution)/shard_map/while/body/eval_jaxpr/jit(_where)/select_n | solution.py:40
  169.7 3.9 %convert_element_type.318 = bf16[8,16,16,512]{3,2,1,0:T(8,128)(2,1)} convert(f32[8,16,16,512]{3,2,1,0:T(8,128)} %get-tuple-element.71) | non-fusion elementwise | flops 1048576 | bytes 6291456 | tf_op jit(solution)/shard_map/convert_element_type | solution.py:56
  173.7 5.0 %collective-permute-start = (bf16[2,128,1,4,128]{4,3,2,1,0:T(4,128)(2,1)S(1)}, bf16[2,128,1,4,128]{4,3,2,1,0:T(4,128)(2,1)S(1)}, u32[]{:S(2)}, u32[]{:S(2)}) collective-permute-start(bf16[2,128,1,4,128]{4,3,2,1,0:T(4,128)(2,1)S(1)} %slice.447), channel_id=1, source_target_pairs={{0,2},{2,4},{4,6},{6,8},{8,10},{10,12},{12,14},{14,16},{16,18},{18... | collective-permute-start | bytes 786440 | tf_op jit(solution)/shard_map/ppermute | solution.py:20
  178.9 5.4 %collective-permute-done = bf16[2,128,1,4,128]{4,3,2,1,0:T(4,128)(2,1)S(1)} collective-permute-done((bf16[2,128,1,4,128]{4,3,2,1,0:T(4,128)(2,1)S(1)}, bf16[2,128,1,4,128]{4,3,2,1,0:T(4,128)(2,1)S(1)}, u32[]{:S(2)}, u32[]{:S(2)}) %collective-permute-start) | collective-permute-done | bytes 262176 | tf_op jit(solution)/shard_map/ppermute | solution.py:20
  186.7 4.4 %slice_convert_fusion.35 = (f32[8,16,1,512]{3,2,1,0:T(1,128)S(1)}, f32[8,16,1,512]{3,2,1,0:T(1,128)S(1)}, f32[8,16,1,512]{3,2,1,0:T(1,128)S(1)}, f32[8,16,1,512]...) fusion(bf16[8,16,16,512]{3,2,1,0:T(8,128)(2,1)S(1)} %copy-done), kind=kLoop, calls=%fused_computation.66 | loop fusion | flops 1048576 | bytes 6291456 | tf_op jit(solution)/shard_map/convert_element_type | solution.py:64
  191.8 3.4 collective-permute-done.1
  196.1 4.6 %collective-permute-start.2 = (bf16[2,128,1,4,128]{4,3,2,1,0:T(4,128)(2,1)S(1)}, bf16[2,128,1,4,128]{4,3,2,1,0:T(4,128)(2,1)S(1)}, u32[]{:S(2)}, u32[]{:S(2)}) collective-permute-start(bf16[2,128,1,4,128]{4,3,2,1,0:T(4,128)(2,1)S(1)} %slice.445), channel_id=1, source_target_pairs={{0,2},{2,4},{4,6},{6,8},{8,10},{10,12},{12,14},{14,16},{16,18},{18... | collective-permute-start | bytes 786440 | tf_op jit(solution)/shard_map/ppermute | solution.py:20
  201.0 3.5 %collective-permute-done.2 = bf16[2,128,1,4,128]{4,3,2,1,0:T(4,128)(2,1)S(1)} collective-permute-done((bf16[2,128,1,4,128]{4,3,2,1,0:T(4,128)(2,1)S(1)}, bf16[2,128,1,4,128]{4,3,2,1,0:T(4,128)(2,1)S(1)}, u32[]{:S(2)}, u32[]{:S(2)}) %collective-permute-start.2) | collective-permute-done | bytes 262176 | tf_op jit(solution)/shard_map/ppermute | solution.py:20
  224.3 2.8 fusion.7
  234.1 2.6 gather_fusion.3
  269.6 18.6 %slice_convert_fusion.19 = (f32[8,16,1,1024]{3,2,1,0:T(1,128)}, f32[8,16,1,1024]{3,2,1,0:T(1,128)}, f32[8,16,1,1024]{3,2,1,0:T(1,128)}, f32[8,16,1,1024]{3,2,1,0...) fusion(bf16[8,16,16,1024]{3,2,1,0:T(8,128)(2,1)} %all-gather.2., ...), kind=kLoop, calls=%fused_computation.50 | loop fusion | flops 2097152 | bytes 12582912 | tf_op jit(solution)/shard_map/convert_element_type | solution.py:64
  288.3 5.7 %multiply_add_fusion = f32[2,128,1,8,128]{4,3,2,1,0:T(8,128)S(1)} fusion(f32[2,128,1,8,128]{4,3,2,1,0:T(8,128)S(1)} %bitcast.314, f32[2,128,1,8,128]{4,3,2,1,0:T(8,128)S(1)} %bitcast.315, f32[2,128,1,8,128]{4,3,2,1,0:T(8,128)S(1)} %bitcast.316, f32[2,128,1,8,128]{4,3,2,1,0:T(8,128)S(1)} %bitcast.317, f32[2,128,1,8,128]{4,3,2,1,0:T(8,128)S(1)} %bitcast.318, ...), kind=kLoop, calls=%fused_computation.28 | loop fusion | flops 8126464 | bytes 26214400 | tf_op jit(solution)/shard_map/add | solution.py:63
  297.4 44.4 %all-reduce.4 = (f32[4,128]{1,0:T(4,128)S(1)}, f32[128]{0:T(128)S(1)}) all-reduce(f32[4,128]{1,0:T(4,128)S(1)} %constant_dynamic-update-slice_fusion, f32[128]{0:T(128)S(1)} %get-tuple-element.95), channel_id=1, replica_groups=mesh['cols'=16,'params'=2] {'cols','params'}, use_global_device_ids=true, to_apply=%region_5.8 | all-reduce | flops 640 | bytes 5120 | tf_op jit(solution)/shard_map/psum | solution.py:124
  (271 shorter events, 137.3 us)
Async XLA Ops:
  7.2 4.4 %copy-start.21 = (s32[128]{0:T(128)S(1)}, s32[128]{0:T(128)}, u32[]{:S(2)}) copy-start(s32[128]{0:T(128)} %param.19) | copy-start | bytes 1540
  7.2 7.6 %copy-start.12 = (f32[8,16,16]{2,1,0:T(8,128)S(1)}, f32[8,16,16]{2,1,0:T(8,128)}, u32[]{:S(2)}) copy-start(f32[8,16,16]{2,1,0:T(8,128)} %param.18) | copy-start | bytes 24580
  7.2 262.3 %all-gather.2.cloned.1.call-start = ((), (), s32[]{:S(2)}) async-start(), calls=%async_computation | async-start | bytes 6291456 | tf_op jit(solution)/shard_map/all_gather | solution.py:114
  7.9 10.5 %copy-start.15 = (s32[1024]{0:T(1024)}, s32[1024]{0:T(1024)S(1)}, u32[]{:S(2)}) copy-start(s32[1024]{0:T(1024)S(1)} %pad_clamp_fusion.1) | copy-start | bytes 12292
  14.6 3.7 %copy-start.16 = (pred[128]{0:T(512)(128)(4,1)}, pred[128]{0:T(512)(128)(4,1)S(1)}, u32[]{:S(2)}) copy-start(pred[128]{0:T(512)(128)(4,1)S(1)} %get-tuple-element.172) | copy-start | bytes 388
  169.6 4.0 %copy-start.1 = (f32[2,128,2,4,128]{4,3,2,1,0:T(4,128)S(1)}, f32[2,128,2,4,128]{4,3,2,1,0:T(4,128)}, u32[]{:S(2)}) copy-start(f32[2,128,2,4,128]{4,3,2,1,0:T(4,128)} %param.20) | copy-start | bytes 3145732
  169.6 9.2 %copy-start.19 = (s32[2,4,128]{2,1,0:T(4,128)S(1)}, s32[2,4,128]{2,1,0:T(4,128)}, u32[]{:S(2)}) copy-start(s32[2,4,128]{2,1,0:T(4,128)} %param.25) | copy-start | bytes 12292
  169.6 9.2 %copy-start.20 = (s32[2,4,128]{2,1,0:T(4,128)S(1)}, s32[2,4,128]{2,1,0:T(4,128)}, u32[]{:S(2)}) copy-start(s32[2,4,128]{2,1,0:T(4,128)} %param.23) | copy-start | bytes 12292
  169.6 14.7 %copy-start.13 = (f32[2,4,128]{2,1,0:T(4,128)S(1)}, f32[2,4,128]{2,1,0:T(4,128)}, u32[]{:S(2)}) copy-start(f32[2,4,128]{2,1,0:T(4,128)} %param.24) | copy-start | bytes 12292
  169.6 14.7 %copy-start.14 = (f32[2,4,128]{2,1,0:T(4,128)S(1)}, f32[2,4,128]{2,1,0:T(4,128)}, u32[]{:S(2)}) copy-start(f32[2,4,128]{2,1,0:T(4,128)} %param.22) | copy-start | bytes 12292
  173.6 13.0 %copy-start = (bf16[8,16,16,512]{3,2,1,0:T(8,128)(2,1)S(1)}, bf16[8,16,16,512]{3,2,1,0:T(8,128)(2,1)}, u32[]{:S(2)}) copy-start(bf16[8,16,16,512]{3,2,1,0:T(8,128)(2,1)} %convert_element_type.318) | copy-start | bytes 6291460
  173.7 10.6 %collective-permute-start = (bf16[2,128,1,4,128]{4,3,2,1,0:T(4,128)(2,1)S(1)}, bf16[2,128,1,4,128]{4,3,2,1,0:T(4,128)(2,1)S(1)}, u32[]{:S(2)}, u32[]{:S(2)}) collective-permute-start(bf16[2,128,1,4,128]{4,3,2,1,0:T(4,128)(2,1)S(1)} %slice.447), channel_id=1, source_target_pairs={{0,2},{2,4},{4,6},{6,8},{8,10},{10,12},{12,14},{14,16},{16,18},{18... | collective-permute-start | bytes 786440 | tf_op jit(solution)/shard_map/ppermute | solution.py:20
  185.4 9.8 %collective-permute-start.1 = (bf16[2,128,1,4,128]{4,3,2,1,0:T(4,128)(2,1)S(1)}, bf16[2,128,1,4,128]{4,3,2,1,0:T(4,128)(2,1)S(1)}, u32[]{:S(2)}, u32[]{:S(2)}) collective-permute-start(bf16[2,128,1,4,128]{4,3,2,1,0:T(4,128)(2,1)S(1)} %slice.446), channel_id=1, source_target_pairs={{2,0},{4,2},{6,4},{8,6},{10,8},{12,10},{14,12},{16,14},{18,16},{20... | collective-permute-start | bytes 786440 | tf_op jit(solution)/shard_map/ppermute | solution.py:20
  196.1 8.4 %collective-permute-start.2 = (bf16[2,128,1,4,128]{4,3,2,1,0:T(4,128)(2,1)S(1)}, bf16[2,128,1,4,128]{4,3,2,1,0:T(4,128)(2,1)S(1)}, u32[]{:S(2)}, u32[]{:S(2)}) collective-permute-start(bf16[2,128,1,4,128]{4,3,2,1,0:T(4,128)(2,1)S(1)} %slice.445), channel_id=1, source_target_pairs={{0,2},{2,4},{4,6},{6,8},{8,10},{10,12},{12,14},{14,16},{16,18},{18... | collective-permute-start | bytes 786440 | tf_op jit(solution)/shard_map/ppermute | solution.py:20
  206.3 24.9 %collective-permute-start.3 = (bf16[2,128,1,4,128]{4,3,2,1,0:T(4,128)(2,1)}, bf16[2,128,1,4,128]{4,3,2,1,0:T(4,128)(2,1)}, u32[]{:S(2)}, u32[]{:S(2)}) collective-permute-start(bf16[2,128,1,4,128]{4,3,2,1,0:T(4,128)(2,1)} %slice.444), channel_id=1, source_target_pairs={{2,0},{4,2},{6,4},{8,6},{10,8},{12,10},{14,12},{16,14},{18,16},{20... | collective-permute-start | bytes 786440 | tf_op jit(solution)/shard_map/ppermute | solution.py:20
  228.7 3.5 %copy-start.11 = (bf16[2,128,2,4,128]{4,3,2,1,0:T(4,128)(2,1)S(1)}, bf16[2,128,2,4,128]{4,3,2,1,0:T(4,128)(2,1)}, u32[]{:S(2)}) copy-start(bf16[2,128,2,4,128]{4,3,2,1,0:T(4,128)(2,1)} %param.21) | copy-start | bytes 1572868
  232.2 4.5 %copy-start.17 = (pred[128]{0:T(512)(128)(4,1)S(1)}, pred[128]{0:T(512)(128)(4,1)}, u32[]{:S(2)}) copy-start(pred[128]{0:T(512)(128)(4,1)} %copy-done.16) | copy-start | bytes 388
  269.5 18.7 %copy-start.2 = (f32[2,128,2,4,128]{4,3,2,1,0:T(4,128)S(1)}, f32[2,128,2,4,128]{4,3,2,1,0:T(4,128)}, u32[]{:S(2)}) copy-start(f32[2,128,2,4,128]{4,3,2,1,0:T(4,128)} %mul.791) | copy-start | bytes 3145732
  269.5 18.7 %copy-start.3 = (f32[2,128,2,4,128]{4,3,2,1,0:T(4,128)S(1)}, f32[2,128,2,4,128]{4,3,2,1,0:T(4,128)}, u32[]{:S(2)}) copy-start(f32[2,128,2,4,128]{4,3,2,1,0:T(4,128)} %mul.786) | copy-start | bytes 3145732
  269.5 18.7 %copy-start.4 = (f32[2,128,2,4,128]{4,3,2,1,0:T(4,128)S(1)}, f32[2,128,2,4,128]{4,3,2,1,0:T(4,128)}, u32[]{:S(2)}) copy-start(f32[2,128,2,4,128]{4,3,2,1,0:T(4,128)} %mul.781) | copy-start | bytes 3145732
  269.5 18.7 %copy-start.5 = (f32[2,128,2,4,128]{4,3,2,1,0:T(4,128)S(1)}, f32[2,128,2,4,128]{4,3,2,1,0:T(4,128)}, u32[]{:S(2)}) copy-start(f32[2,128,2,4,128]{4,3,2,1,0:T(4,128)} %mul.776) | copy-start | bytes 3145732
  269.5 18.7 %copy-start.6 = (f32[2,128,2,4,128]{4,3,2,1,0:T(4,128)S(1)}, f32[2,128,2,4,128]{4,3,2,1,0:T(4,128)}, u32[]{:S(2)}) copy-start(f32[2,128,2,4,128]{4,3,2,1,0:T(4,128)} %mul.771) | copy-start | bytes 3145732
  269.5 18.7 %copy-start.7 = (f32[2,128,2,4,128]{4,3,2,1,0:T(4,128)S(1)}, f32[2,128,2,4,128]{4,3,2,1,0:T(4,128)}, u32[]{:S(2)}) copy-start(f32[2,128,2,4,128]{4,3,2,1,0:T(4,128)} %mul.766) | copy-start | bytes 3145732
  269.5 18.7 %copy-start.8 = (f32[2,128,2,4,128]{4,3,2,1,0:T(4,128)S(1)}, f32[2,128,2,4,128]{4,3,2,1,0:T(4,128)}, u32[]{:S(2)}) copy-start(f32[2,128,2,4,128]{4,3,2,1,0:T(4,128)} %mul.761) | copy-start | bytes 3145732
  269.5 18.7 %copy-start.9 = (f32[2,128,2,4,128]{4,3,2,1,0:T(4,128)S(1)}, f32[2,128,2,4,128]{4,3,2,1,0:T(4,128)}, u32[]{:S(2)}) copy-start(f32[2,128,2,4,128]{4,3,2,1,0:T(4,128)} %mul.756) | copy-start | bytes 3145732
  269.5 18.7 %copy-start.10 = (f32[2,128,2,4,128]{4,3,2,1,0:T(4,128)S(1)}, f32[2,128,2,4,128]{4,3,2,1,0:T(4,128)}, u32[]{:S(2)}) copy-start(f32[2,128,2,4,128]{4,3,2,1,0:T(4,128)} %mul.751) | copy-start | bytes 3145732
  288.3 7.0 %copy-start.18 = (pred[128]{0:T(512)(128)(4,1)S(1)}, pred[128]{0:T(512)(128)(4,1)}, u32[]{:S(2)}) copy-start(pred[128]{0:T(512)(128)(4,1)} %get-tuple-element.171) | copy-start | bytes 388
Sparse Core Ops, SparseCore 0:
  173.7 16.3 all-gather.1
where the time goes:
time: 352 us; the launch traced here: 350 us
  other arithmetic  204 us (58%)
  local copies, waits for them, and re-layouts  61.1 us (17%)
  blocking collectives  44.4 us (13%)
  between operations  14.8 us (4%)
  starting transfers between devices  12.4 us (4%)
  waiting for transfers between devices  12.3 us (3%)
    select_n x16, other arithmetic, eliminate(): jnp.where((positions == pivot_index)[None, :, None, None], pivot_row[:, N...  85.5 us
    psum x1, blocking collectives, shards(): lax.psum((row_table, partial_conc), ('cols', 'params'))  44.4 us
    mul x16, other arithmetic, eliminate(): -column[:, :, None, :] * pivot[:, None, None, :]  32.7 us
    mul x49, local copies, waits for them, and re-layouts, apply_blocks(): factors[:, :, column_index, :].astype(jnp.float32)[None]  31.5 us
    convert_element_type x2, other arithmetic, apply_blocks(): factors[:, :, column_index, :].astype(jnp.float32)[None]  23.1 us
    unnamed x77, local copies, waits for them, and re-layouts  17.2 us
    broadcast_in_dim x16, other arithmetic, eliminate(): jnp.where((positions == pivot_index)[None, :, None, None], pivot_row[:, N...  16.8 us
    div x16, other arithmetic, eliminate(): pivot = 1.0 / current[:, pivot_index, pivot_index, :]  14.9 us
  transfers between devices with their start and end apart: 5, of which 3 were waited for; matrix products, arithmetic and copies ran while one was open for 20% of the time, Pallas kernels for 0%

commit v1 on v0

--- a/solution.py
+++ b/solution.py
@@ -121,7 +121,7 @@
     group_index = lax.axis_index("params")
     row_table = jnp.zeros((groups * lax.axis_size("params"), species), jnp.float32)
     row_table = lax.dynamic_update_slice(row_table, partial_sens, (group_index * groups, 0))
-    table_total, conc_total = lax.psum((row_table, partial_conc), ("cols", "params"))
+    table_total, conc_total = lax.psum(lax.psum((row_table, partial_conc), "params"), "cols")
     sens_total = lax.dynamic_slice(table_total, (group_index * groups, 0), (groups, species))
     return (new_concentration, new_sensitivity, sens_total / total_cells, conc_total / total_cells)
 

time: 352 us -> 356 us (1.011)
  blocking collectives: 44.4 us -> 48 us
    psum x1 -> x2, blocking collectives: 44.4 us -> 48 us  [the longest x1 45.6 us: shards(): lax.psum(lax.psum((row_table, partial_conc), 'params'), 'cols')]
where the time goes in v1:
time: 356 us; the launch traced here: 353 us
  other arithmetic  204 us (57%)
  local copies, waits for them, and re-layouts  61 us (17%)
  blocking collectives  48 us (13%)
  between operations  14.8 us (4%)
  starting transfers between devices  12.4 us (3%)
  waiting for transfers between devices  12.3 us (3%)
    select_n x16, other arithmetic, eliminate(): jnp.where((positions == pivot_index)[None, :, None, None], pivot_row[:, N...  85.4 us
    psum x1, blocking collectives, shards(): lax.psum(lax.psum((row_table, partial_conc), 'params'), 'cols')  45.6 us
    mul x16, other arithmetic, eliminate(): -column[:, :, None, :] * pivot[:, None, None, :]  32.7 us
    mul x49, local copies, waits for them, and re-layouts, apply_blocks(): factors[:, :, column_index, :].astype(jnp.float32)[None]  31.5 us
    convert_element_type x2, other arithmetic, apply_blocks(): factors[:, :, column_index, :].astype(jnp.float32)[None]  23.2 us
    unnamed x77, local copies, waits for them, and re-layouts  17.1 us
    broadcast_in_dim x16, other arithmetic, eliminate(): jnp.where((positions == pivot_index)[None, :, None, None], pivot_row[:, N...  16.8 us
    div x16, other arithmetic, eliminate(): pivot = 1.0 / current[:, pivot_index, pivot_index, :]  14.9 us
  transfers between devices with their start and end apart: 5, of which 3 were waited for; matrix products, arithmetic and copies ran while one was open for 20% of the time, Pallas kernels for 0%

profile of v1, /device:TPU:0, one launch (start us, length us, event | category | flops | bytes accessed | tf_op | source)
XLA Modules:
  0.0 353.3 jit_solution(18159750587518300421)
XLA Ops:
  11.6 2.5 sort.17
  15.8 2.5 multiply_subtract_fusion
  18.4 151.1 %while.14 = (s32[]{:T(128)}, f32[8,16,16,512]{3,2,1,0:T(8,128)}, s32[]{:T(128)}) while((s32[]{:T(128)}, f32[8,16,16,512]{3,2,1,0:T(8,128)}, s32[]{:T(128)}) %tuple.112), condition=%wide.region_2.4_spmd.clone, body=%wide.region_1.3_spmd.clone.sunk | while | flops 4460562 | bytes 11632757 | solution.py:45
  22.5 5.3 %select_select_fusion.2 = f32[8,16,16,512]{3,2,1,0:T(8,128)} fusion(f32[8,16,16,512]{3,2,1,0:T(8,128)} %get-tuple-element.202, f32[8,16,512]{2,1,0:T(8,128)S(1)} %get-tuple-element.196, f32[8,16,512]{2,1,0:T(8,128)S(1)} %get-tuple-element.197, f32[8,16,512]{2,1,0:T(8,128)S(1)} %select_bitcast_fusion.5, pred[16]{0:T(512)(128)(4,1)S(1)} %iota_compare_fusion.3), kind=kLoop, calls=%fused_computation.6.clone.1 | loop fusion | flops 4194304 | bytes 9175056 | tf_op jit(solution)/shard_map/while/body/eval_jaxpr/jit(_where)/select_n | solution.py:40
  31.9 5.3 %select_select_fusion.2 = f32[8,16,16,512]{3,2,1,0:T(8,128)} fusion(f32[8,16,16,512]{3,2,1,0:T(8,128)} %get-tuple-element.202, f32[8,16,512]{2,1,0:T(8,128)S(1)} %get-tuple-element.196, f32[8,16,512]{2,1,0:T(8,128)S(1)} %get-tuple-element.197, f32[8,16,512]{2,1,0:T(8,128)S(1)} %select_bitcast_fusion.5, pred[16]{0:T(512)(128)(4,1)S(1)} %iota_compare_fusion.3), kind=kLoop, calls=%fused_computation.6.clone.1 | loop fusion | flops 4194304 | bytes 9175056 | tf_op jit(solution)/shard_map/while/body/eval_jaxpr/jit(_where)/select_n | solution.py:40
  41.4 5.3 %select_select_fusion.2 = f32[8,16,16,512]{3,2,1,0:T(8,128)} fusion(f32[8,16,16,512]{3,2,1,0:T(8,128)} %get-tuple-element.202, f32[8,16,512]{2,1,0:T(8,128)S(1)} %get-tuple-element.196, f32[8,16,512]{2,1,0:T(8,128)S(1)} %get-tuple-element.197, f32[8,16,512]{2,1,0:T(8,128)S(1)} %select_bitcast_fusion.5, pred[16]{0:T(512)(128)(4,1)S(1)} %iota_compare_fusion.3), kind=kLoop, calls=%fused_computation.6.clone.1 | loop fusion | flops 4194304 | bytes 9175056 | tf_op jit(solution)/shard_map/while/body/eval_jaxpr/jit(_where)/select_n | solution.py:40
  50.8 5.3 %select_select_fusion.2 = f32[8,16,16,512]{3,2,1,0:T(8,128)} fusion(f32[8,16,16,512]{3,2,1,0:T(8,128)} %get-tuple-element.202, f32[8,16,512]{2,1,0:T(8,128)S(1)} %get-tuple-element.196, f32[8,16,512]{2,1,0:T(8,128)S(1)} %get-tuple-element.197, f32[8,16,512]{2,1,0:T(8,128)S(1)} %select_bitcast_fusion.5, pred[16]{0:T(512)(128)(4,1)S(1)} %iota_compare_fusion.3), kind=kLoop, calls=%fused_computation.6.clone.1 | loop fusion | flops 4194304 | bytes 9175056 | tf_op jit(solution)/shard_map/while/body/eval_jaxpr/jit(_where)/select_n | solution.py:40
  60.3 5.3 %select_select_fusion.2 = f32[8,16,16,512]{3,2,1,0:T(8,128)} fusion(f32[8,16,16,512]{3,2,1,0:T(8,128)} %get-tuple-element.202, f32[8,16,512]{2,1,0:T(8,128)S(1)} %get-tuple-element.196, f32[8,16,512]{2,1,0:T(8,128)S(1)} %get-tuple-element.197, f32[8,16,512]{2,1,0:T(8,128)S(1)} %select_bitcast_fusion.5, pred[16]{0:T(512)(128)(4,1)S(1)} %iota_compare_fusion.3), kind=kLoop, calls=%fused_computation.6.clone.1 | loop fusion | flops 4194304 | bytes 9175056 | tf_op jit(solution)/shard_map/while/body/eval_jaxpr/jit(_where)/select_n | solution.py:40
  69.7 5.3 %select_select_fusion.2 = f32[8,16,16,512]{3,2,1,0:T(8,128)} fusion(f32[8,16,16,512]{3,2,1,0:T(8,128)} %get-tuple-element.202, f32[8,16,512]{2,1,0:T(8,128)S(1)} %get-tuple-element.196, f32[8,16,512]{2,1,0:T(8,128)S(1)} %get-tuple-element.197, f32[8,16,512]{2,1,0:T(8,128)S(1)} %select_bitcast_fusion.5, pred[16]{0:T(512)(128)(4,1)S(1)} %iota_compare_fusion.3), kind=kLoop, calls=%fused_computation.6.clone.1 | loop fusion | flops 4194304 | bytes 9175056 | tf_op jit(solution)/shard_map/while/body/eval_jaxpr/jit(_where)/select_n | solution.py:40
  79.1 5.3 %select_select_fusion.2 = f32[8,16,16,512]{3,2,1,0:T(8,128)} fusion(f32[8,16,16,512]{3,2,1,0:T(8,128)} %get-tuple-element.202, f32[8,16,512]{2,1,0:T(8,128)S(1)} %get-tuple-element.196, f32[8,16,512]{2,1,0:T(8,128)S(1)} %get-tuple-element.197, f32[8,16,512]{2,1,0:T(8,128)S(1)} %select_bitcast_fusion.5, pred[16]{0:T(512)(128)(4,1)S(1)} %iota_compare_fusion.3), kind=kLoop, calls=%fused_computation.6.clone.1 | loop fusion | flops 4194304 | bytes 9175056 | tf_op jit(solution)/shard_map/while/body/eval_jaxpr/jit(_where)/select_n | solution.py:40
  88.6 5.3 %select_select_fusion.2 = f32[8,16,16,512]{3,2,1,0:T(8,128)} fusion(f32[8,16,16,512]{3,2,1,0:T(8,128)} %get-tuple-element.202, f32[8,16,512]{2,1,0:T(8,128)S(1)} %get-tuple-element.196, f32[8,16,512]{2,1,0:T(8,128)S(1)} %get-tuple-element.197, f32[8,16,512]{2,1,0:T(8,128)S(1)} %select_bitcast_fusion.5, pred[16]{0:T(512)(128)(4,1)S(1)} %iota_compare_fusion.3), kind=kLoop, calls=%fused_computation.6.clone.1 | loop fusion | flops 4194304 | bytes 9175056 | tf_op jit(solution)/shard_map/while/body/eval_jaxpr/jit(_where)/select_n | solution.py:40
  98.0 5.3 %select_select_fusion.2 = f32[8,16,16,512]{3,2,1,0:T(8,128)} fusion(f32[8,16,16,512]{3,2,1,0:T(8,128)} %get-tuple-element.202, f32[8,16,512]{2,1,0:T(8,128)S(1)} %get-tuple-element.196, f32[8,16,512]{2,1,0:T(8,128)S(1)} %get-tuple-element.197, f32[8,16,512]{2,1,0:T(8,128)S(1)} %select_bitcast_fusion.5, pred[16]{0:T(512)(128)(4,1)S(1)} %iota_compare_fusion.3), kind=kLoop, calls=%fused_computation.6.clone.1 | loop fusion | flops 4194304 | bytes 9175056 | tf_op jit(solution)/shard_map/while/body/eval_jaxpr/jit(_where)/select_n | solution.py:40
  107.5 5.3 %select_select_fusion.2 = f32[8,16,16,512]{3,2,1,0:T(8,128)} fusion(f32[8,16,16,512]{3,2,1,0:T(8,128)} %get-tuple-element.202, f32[8,16,512]{2,1,0:T(8,128)S(1)} %get-tuple-element.196, f32[8,16,512]{2,1,0:T(8,128)S(1)} %get-tuple-element.197, f32[8,16,512]{2,1,0:T(8,128)S(1)} %select_bitcast_fusion.5, pred[16]{0:T(512)(128)(4,1)S(1)} %iota_compare_fusion.3), kind=kLoop, calls=%fused_computation.6.clone.1 | loop fusion | flops 4194304 | bytes 9175056 | tf_op jit(solution)/shard_map/while/body/eval_jaxpr/jit(_where)/select_n | solution.py:40
  116.9 5.3 %select_select_fusion.2 = f32[8,16,16,512]{3,2,1,0:T(8,128)} fusion(f32[8,16,16,512]{3,2,1,0:T(8,128)} %get-tuple-element.202, f32[8,16,512]{2,1,0:T(8,128)S(1)} %get-tuple-element.196, f32[8,16,512]{2,1,0:T(8,128)S(1)} %get-tuple-element.197, f32[8,16,512]{2,1,0:T(8,128)S(1)} %select_bitcast_fusion.5, pred[16]{0:T(512)(128)(4,1)S(1)} %iota_compare_fusion.3), kind=kLoop, calls=%fused_computation.6.clone.1 | loop fusion | flops 4194304 | bytes 9175056 | tf_op jit(solution)/shard_map/while/body/eval_jaxpr/jit(_where)/select_n | solution.py:40
  126.4 5.3 %select_select_fusion.2 = f32[8,16,16,512]{3,2,1,0:T(8,128)} fusion(f32[8,16,16,512]{3,2,1,0:T(8,128)} %get-tuple-element.202, f32[8,16,512]{2,1,0:T(8,128)S(1)} %get-tuple-element.196, f32[8,16,512]{2,1,0:T(8,128)S(1)} %get-tuple-element.197, f32[8,16,512]{2,1,0:T(8,128)S(1)} %select_bitcast_fusion.5, pred[16]{0:T(512)(128)(4,1)S(1)} %iota_compare_fusion.3), kind=kLoop, calls=%fused_computation.6.clone.1 | loop fusion | flops 4194304 | bytes 9175056 | tf_op jit(solution)/shard_map/while/body/eval_jaxpr/jit(_where)/select_n | solution.py:40
  135.8 5.3 %select_select_fusion.2 = f32[8,16,16,512]{3,2,1,0:T(8,128)} fusion(f32[8,16,16,512]{3,2,1,0:T(8,128)} %get-tuple-element.202, f32[8,16,512]{2,1,0:T(8,128)S(1)} %get-tuple-element.196, f32[8,16,512]{2,1,0:T(8,128)S(1)} %get-tuple-element.197, f32[8,16,512]{2,1,0:T(8,128)S(1)} %select_bitcast_fusion.5, pred[16]{0:T(512)(128)(4,1)S(1)} %iota_compare_fusion.3), kind=kLoop, calls=%fused_computation.6.clone.1 | loop fusion | flops 4194304 | bytes 9175056 | tf_op jit(solution)/shard_map/while/body/eval_jaxpr/jit(_where)/select_n | solution.py:40
  145.3 5.3 %select_select_fusion.2 = f32[8,16,16,512]{3,2,1,0:T(8,128)} fusion(f32[8,16,16,512]{3,2,1,0:T(8,128)} %get-tuple-element.202, f32[8,16,512]{2,1,0:T(8,128)S(1)} %get-tuple-element.196, f32[8,16,512]{2,1,0:T(8,128)S(1)} %get-tuple-element.197, f32[8,16,512]{2,1,0:T(8,128)S(1)} %select_bitcast_fusion.5, pred[16]{0:T(512)(128)(4,1)S(1)} %iota_compare_fusion.3), kind=kLoop, calls=%fused_computation.6.clone.1 | loop fusion | flops 4194304 | bytes 9175056 | tf_op jit(solution)/shard_map/while/body/eval_jaxpr/jit(_where)/select_n | solution.py:40
  154.7 5.3 %select_select_fusion.2 = f32[8,16,16,512]{3,2,1,0:T(8,128)} fusion(f32[8,16,16,512]{3,2,1,0:T(8,128)} %get-tuple-element.202, f32[8,16,512]{2,1,0:T(8,128)S(1)} %get-tuple-element.196, f32[8,16,512]{2,1,0:T(8,128)S(1)} %get-tuple-element.197, f32[8,16,512]{2,1,0:T(8,128)S(1)} %select_bitcast_fusion.5, pred[16]{0:T(512)(128)(4,1)S(1)} %iota_compare_fusion.3), kind=kLoop, calls=%fused_computation.6.clone.1 | loop fusion | flops 4194304 | bytes 9175056 | tf_op jit(solution)/shard_map/while/body/eval_jaxpr/jit(_where)/select_n | solution.py:40
  164.1 5.3 %select_select_fusion.2 = f32[8,16,16,512]{3,2,1,0:T(8,128)} fusion(f32[8,16,16,512]{3,2,1,0:T(8,128)} %get-tuple-element.202, f32[8,16,512]{2,1,0:T(8,128)S(1)} %get-tuple-element.196, f32[8,16,512]{2,1,0:T(8,128)S(1)} %get-tuple-element.197, f32[8,16,512]{2,1,0:T(8,128)S(1)} %select_bitcast_fusion.5, pred[16]{0:T(512)(128)(4,1)S(1)} %iota_compare_fusion.3), kind=kLoop, calls=%fused_computation.6.clone.1 | loop fusion | flops 4194304 | bytes 9175056 | tf_op jit(solution)/shard_map/while/body/eval_jaxpr/jit(_where)/select_n | solution.py:40
  169.5 4.0 %convert_element_type.318 = bf16[8,16,16,512]{3,2,1,0:T(8,128)(2,1)} convert(f32[8,16,16,512]{3,2,1,0:T(8,128)} %get-tuple-element.71) | non-fusion elementwise | flops 1048576 | bytes 6291456 | tf_op jit(solution)/shard_map/convert_element_type | solution.py:56
  173.6 5.0 %collective-permute-start = (bf16[2,128,1,4,128]{4,3,2,1,0:T(4,128)(2,1)S(1)}, bf16[2,128,1,4,128]{4,3,2,1,0:T(4,128)(2,1)S(1)}, u32[]{:S(2)}, u32[]{:S(2)}) collective-permute-start(bf16[2,128,1,4,128]{4,3,2,1,0:T(4,128)(2,1)S(1)} %slice.447), channel_id=1, source_target_pairs={{0,2},{2,4},{4,6},{6,8},{8,10},{10,12},{12,14},{14,16},{16,18},{18... | collective-permute-start | bytes 786440 | tf_op jit(solution)/shard_map/ppermute | solution.py:20
  178.8 5.4 %collective-permute-done = bf16[2,128,1,4,128]{4,3,2,1,0:T(4,128)(2,1)S(1)} collective-permute-done((bf16[2,128,1,4,128]{4,3,2,1,0:T(4,128)(2,1)S(1)}, bf16[2,128,1,4,128]{4,3,2,1,0:T(4,128)(2,1)S(1)}, u32[]{:S(2)}, u32[]{:S(2)}) %collective-permute-start) | collective-permute-done | bytes 262176 | tf_op jit(solution)/shard_map/ppermute | solution.py:20
  186.5 4.4 %slice_convert_fusion.35 = (f32[8,16,1,512]{3,2,1,0:T(1,128)S(1)}, f32[8,16,1,512]{3,2,1,0:T(1,128)S(1)}, f32[8,16,1,512]{3,2,1,0:T(1,128)S(1)}, f32[8,16,1,512]...) fusion(bf16[8,16,16,512]{3,2,1,0:T(8,128)(2,1)S(1)} %copy-done), kind=kLoop, calls=%fused_computation.66 | loop fusion | flops 1048576 | bytes 6291456 | tf_op jit(solution)/shard_map/convert_element_type | solution.py:64
  191.7 3.4 collective-permute-done.1
  195.9 4.6 %collective-permute-start.2 = (bf16[2,128,1,4,128]{4,3,2,1,0:T(4,128)(2,1)S(1)}, bf16[2,128,1,4,128]{4,3,2,1,0:T(4,128)(2,1)S(1)}, u32[]{:S(2)}, u32[]{:S(2)}) collective-permute-start(bf16[2,128,1,4,128]{4,3,2,1,0:T(4,128)(2,1)S(1)} %slice.445), channel_id=1, source_target_pairs={{0,2},{2,4},{4,6},{6,8},{8,10},{10,12},{12,14},{14,16},{16,18},{18... | collective-permute-start | bytes 786440 | tf_op jit(solution)/shard_map/ppermute | solution.py:20
  200.9 3.5 collective-permute-done.2
  224.2 2.8 fusion.7
  234.0 2.6 gather_fusion.3
  269.3 18.8 %slice_convert_fusion.19 = (f32[8,16,1,1024]{3,2,1,0:T(1,128)}, f32[8,16,1,1024]{3,2,1,0:T(1,128)}, f32[8,16,1,1024]{3,2,1,0:T(1,128)}, f32[8,16,1,1024]{3,2,1,0...) fusion(bf16[8,16,16,1024]{3,2,1,0:T(8,128)(2,1)} %all-gather.2., ...), kind=kLoop, calls=%fused_computation.50 | loop fusion | flops 2097152 | bytes 12582912 | tf_op jit(solution)/shard_map/convert_element_type | solution.py:64
  288.3 5.7 %multiply_add_fusion = f32[2,128,1,8,128]{4,3,2,1,0:T(8,128)S(1)} fusion(f32[2,128,1,8,128]{4,3,2,1,0:T(8,128)S(1)} %bitcast.314, f32[2,128,1,8,128]{4,3,2,1,0:T(8,128)S(1)} %bitcast.315, f32[2,128,1,8,128]{4,3,2,1,0:T(8,128)S(1)} %bitcast.316, f32[2,128,1,8,128]{4,3,2,1,0:T(8,128)S(1)} %bitcast.317, f32[2,128,1,8,128]{4,3,2,1,0:T(8,128)S(1)} %bitcast.318, ...), kind=kLoop, calls=%fused_computation.28 | loop fusion | flops 8126464 | bytes 26214400 | tf_op jit(solution)/shard_map/add | solution.py:63
  297.3 2.5 all-reduce.5
  299.8 45.6 %all-reduce.4 = (f32[4,128]{1,0:T(4,128)S(1)}, f32[128]{0:T(128)S(1)}) all-reduce(f32[4,128]{1,0:T(4,128)S(1)} %get-tuple-element.93, f32[128]{0:T(128)S(1)} %get-tuple-element.94), channel_id=1, replica_groups=mesh['cols'=16,'params'=2] {'cols'}, use_global_device_ids=true, to_apply=%region_6.9 | all-reduce | flops 640 | bytes 5120 | tf_op jit(solution)/shard_map/psum | solution.py:124
  (272 shorter events, 139.3 us)
Async XLA Ops:
  7.2 4.4 %copy-start.21 = (s32[128]{0:T(128)S(1)}, s32[128]{0:T(128)}, u32[]{:S(2)}) copy-start(s32[128]{0:T(128)} %param.19) | copy-start | bytes 1540
  7.2 7.6 %copy-start.12 = (f32[8,16,16]{2,1,0:T(8,128)S(1)}, f32[8,16,16]{2,1,0:T(8,128)}, u32[]{:S(2)}) copy-start(f32[8,16,16]{2,1,0:T(8,128)} %param.18) | copy-start | bytes 24580
  7.2 262.1 %all-gather.2.cloned.1.call-start = ((), (), s32[]{:S(2)}) async-start(), calls=%async_computation | async-start | bytes 6291456 | tf_op jit(solution)/shard_map/all_gather | solution.py:114
  7.9 10.5 %copy-start.15 = (s32[1024]{0:T(1024)}, s32[1024]{0:T(1024)S(1)}, u32[]{:S(2)}) copy-start(s32[1024]{0:T(1024)S(1)} %pad_clamp_fusion.1) | copy-start | bytes 12292
  14.6 3.7 %copy-start.16 = (pred[128]{0:T(512)(128)(4,1)}, pred[128]{0:T(512)(128)(4,1)S(1)}, u32[]{:S(2)}) copy-start(pred[128]{0:T(512)(128)(4,1)S(1)} %get-tuple-element.174) | copy-start | bytes 388
  169.5 4.0 %copy-start.1 = (f32[2,128,2,4,128]{4,3,2,1,0:T(4,128)S(1)}, f32[2,128,2,4,128]{4,3,2,1,0:T(4,128)}, u32[]{:S(2)}) copy-start(f32[2,128,2,4,128]{4,3,2,1,0:T(4,128)} %param.20) | copy-start | bytes 3145732
  169.5 9.2 %copy-start.19 = (s32[2,4,128]{2,1,0:T(4,128)S(1)}, s32[2,4,128]{2,1,0:T(4,128)}, u32[]{:S(2)}) copy-start(s32[2,4,128]{2,1,0:T(4,128)} %param.25) | copy-start | bytes 12292
  169.5 9.3 %copy-start.20 = (s32[2,4,128]{2,1,0:T(4,128)S(1)}, s32[2,4,128]{2,1,0:T(4,128)}, u32[]{:S(2)}) copy-start(s32[2,4,128]{2,1,0:T(4,128)} %param.23) | copy-start | bytes 12292
  169.5 14.7 %copy-start.13 = (f32[2,4,128]{2,1,0:T(4,128)S(1)}, f32[2,4,128]{2,1,0:T(4,128)}, u32[]{:S(2)}) copy-start(f32[2,4,128]{2,1,0:T(4,128)} %param.24) | copy-start | bytes 12292
  169.5 14.7 %copy-start.14 = (f32[2,4,128]{2,1,0:T(4,128)S(1)}, f32[2,4,128]{2,1,0:T(4,128)}, u32[]{:S(2)}) copy-start(f32[2,4,128]{2,1,0:T(4,128)} %param.22) | copy-start | bytes 12292
  173.5 13.0 %copy-start = (bf16[8,16,16,512]{3,2,1,0:T(8,128)(2,1)S(1)}, bf16[8,16,16,512]{3,2,1,0:T(8,128)(2,1)}, u32[]{:S(2)}) copy-start(bf16[8,16,16,512]{3,2,1,0:T(8,128)(2,1)} %convert_element_type.318) | copy-start | bytes 6291460
  173.6 10.6 %collective-permute-start = (bf16[2,128,1,4,128]{4,3,2,1,0:T(4,128)(2,1)S(1)}, bf16[2,128,1,4,128]{4,3,2,1,0:T(4,128)(2,1)S(1)}, u32[]{:S(2)}, u32[]{:S(2)}) collective-permute-start(bf16[2,128,1,4,128]{4,3,2,1,0:T(4,128)(2,1)S(1)} %slice.447), channel_id=1, source_target_pairs={{0,2},{2,4},{4,6},{6,8},{8,10},{10,12},{12,14},{14,16},{16,18},{18... | collective-permute-start | bytes 786440 | tf_op jit(solution)/shard_map/ppermute | solution.py:20
  185.2 9.8 %collective-permute-start.1 = (bf16[2,128,1,4,128]{4,3,2,1,0:T(4,128)(2,1)S(1)}, bf16[2,128,1,4,128]{4,3,2,1,0:T(4,128)(2,1)S(1)}, u32[]{:S(2)}, u32[]{:S(2)}) collective-permute-start(bf16[2,128,1,4,128]{4,3,2,1,0:T(4,128)(2,1)S(1)} %slice.446), channel_id=1, source_target_pairs={{2,0},{4,2},{6,4},{8,6},{10,8},{12,10},{14,12},{16,14},{18,16},{20... | collective-permute-start | bytes 786440 | tf_op jit(solution)/shard_map/ppermute | solution.py:20
  195.9 8.4 %collective-permute-start.2 = (bf16[2,128,1,4,128]{4,3,2,1,0:T(4,128)(2,1)S(1)}, bf16[2,128,1,4,128]{4,3,2,1,0:T(4,128)(2,1)S(1)}, u32[]{:S(2)}, u32[]{:S(2)}) collective-permute-start(bf16[2,128,1,4,128]{4,3,2,1,0:T(4,128)(2,1)S(1)} %slice.445), channel_id=1, source_target_pairs={{0,2},{2,4},{4,6},{6,8},{8,10},{10,12},{12,14},{14,16},{16,18},{18... | collective-permute-start | bytes 786440 | tf_op jit(solution)/shard_map/ppermute | solution.py:20
  206.1 24.9 %collective-permute-start.3 = (bf16[2,128,1,4,128]{4,3,2,1,0:T(4,128)(2,1)}, bf16[2,128,1,4,128]{4,3,2,1,0:T(4,128)(2,1)}, u32[]{:S(2)}, u32[]{:S(2)}) collective-permute-start(bf16[2,128,1,4,128]{4,3,2,1,0:T(4,128)(2,1)} %slice.444), channel_id=1, source_target_pairs={{2,0},{4,2},{6,4},{8,6},{10,8},{12,10},{14,12},{16,14},{18,16},{20... | collective-permute-start | bytes 786440 | tf_op jit(solution)/shard_map/ppermute | solution.py:20
  228.5 3.5 copy-start.11
  232.0 4.5 %copy-start.17 = (pred[128]{0:T(512)(128)(4,1)S(1)}, pred[128]{0:T(512)(128)(4,1)}, u32[]{:S(2)}) copy-start(pred[128]{0:T(512)(128)(4,1)} %copy-done.16) | copy-start | bytes 388
  269.3 18.9 %copy-start.2 = (f32[2,128,2,4,128]{4,3,2,1,0:T(4,128)S(1)}, f32[2,128,2,4,128]{4,3,2,1,0:T(4,128)}, u32[]{:S(2)}) copy-start(f32[2,128,2,4,128]{4,3,2,1,0:T(4,128)} %mul.791) | copy-start | bytes 3145732
  269.3 18.9 %copy-start.3 = (f32[2,128,2,4,128]{4,3,2,1,0:T(4,128)S(1)}, f32[2,128,2,4,128]{4,3,2,1,0:T(4,128)}, u32[]{:S(2)}) copy-start(f32[2,128,2,4,128]{4,3,2,1,0:T(4,128)} %mul.786) | copy-start | bytes 3145732
  269.3 18.9 %copy-start.4 = (f32[2,128,2,4,128]{4,3,2,1,0:T(4,128)S(1)}, f32[2,128,2,4,128]{4,3,2,1,0:T(4,128)}, u32[]{:S(2)}) copy-start(f32[2,128,2,4,128]{4,3,2,1,0:T(4,128)} %mul.781) | copy-start | bytes 3145732
  269.3 18.9 %copy-start.5 = (f32[2,128,2,4,128]{4,3,2,1,0:T(4,128)S(1)}, f32[2,128,2,4,128]{4,3,2,1,0:T(4,128)}, u32[]{:S(2)}) copy-start(f32[2,128,2,4,128]{4,3,2,1,0:T(4,128)} %mul.776) | copy-start | bytes 3145732
  269.3 18.9 %copy-start.6 = (f32[2,128,2,4,128]{4,3,2,1,0:T(4,128)S(1)}, f32[2,128,2,4,128]{4,3,2,1,0:T(4,128)}, u32[]{:S(2)}) copy-start(f32[2,128,2,4,128]{4,3,2,1,0:T(4,128)} %mul.771) | copy-start | bytes 3145732
  269.3 18.9 %copy-start.7 = (f32[2,128,2,4,128]{4,3,2,1,0:T(4,128)S(1)}, f32[2,128,2,4,128]{4,3,2,1,0:T(4,128)}, u32[]{:S(2)}) copy-start(f32[2,128,2,4,128]{4,3,2,1,0:T(4,128)} %mul.766) | copy-start | bytes 3145732
  269.3 18.9 %copy-start.8 = (f32[2,128,2,4,128]{4,3,2,1,0:T(4,128)S(1)}, f32[2,128,2,4,128]{4,3,2,1,0:T(4,128)}, u32[]{:S(2)}) copy-start(f32[2,128,2,4,128]{4,3,2,1,0:T(4,128)} %mul.761) | copy-start | bytes 3145732
  269.3 18.9 %copy-start.9 = (f32[2,128,2,4,128]{4,3,2,1,0:T(4,128)S(1)}, f32[2,128,2,4,128]{4,3,2,1,0:T(4,128)}, u32[]{:S(2)}) copy-start(f32[2,128,2,4,128]{4,3,2,1,0:T(4,128)} %mul.756) | copy-start | bytes 3145732
  269.3 18.9 %copy-start.10 = (f32[2,128,2,4,128]{4,3,2,1,0:T(4,128)S(1)}, f32[2,128,2,4,128]{4,3,2,1,0:T(4,128)}, u32[]{:S(2)}) copy-start(f32[2,128,2,4,128]{4,3,2,1,0:T(4,128)} %mul.751) | copy-start | bytes 3145732
  288.2 7.0 %copy-start.18 = (pred[128]{0:T(512)(128)(4,1)S(1)}, pred[128]{0:T(512)(128)(4,1)}, u32[]{:S(2)}) copy-start(pred[128]{0:T(512)(128)(4,1)} %get-tuple-element.173) | copy-start | bytes 388
Sparse Core Ops, SparseCore 0:
  173.6 16.3 all-gather.1
